TPU v7x, 256 devices: a whole 4x4x8 slice. The times are simulated.
256 devices in a mesh: row: 16 (over z, core), col: 8 (over x_hi, y), feat: 2 (over x_lo).
Axes of the slice: x: 4 (x_hi: 2, x_lo: 2; x = x_hi * 2 + x_lo), y: 4, z: 8, core: 2. Of those that a mesh axis runs over, the one named last changes fastest.
Arguments:
- features: bfloat16 [65536, 256], P(('col', 'row'), 'feat'), may hold values from -6 to 6
- tile_rows: int32 [16, 8, 256], P('row', 'col'), may hold values from 0 to 31, as said below
- tile_cols: int32 [16, 8, 256], P('row', 'col'), may hold values from 0 to 63
- tile_count: int32 [16, 8], P('row', 'col'), may hold values from 64 to 256, as said below
- tile_values: bfloat16 [16, 8, 256, 128, 128], P('row', 'col'), may hold values from -0.21875 to 0.21875
- weights: bfloat16 [256, 256], replicated, may hold values from -0.375 to 0.375
- cotangent: bfloat16 [65536, 256], P(('row', 'col'), 'feat'), may hold values from -6 to 6
Outputs:
- activated: bfloat16 [65536, 256], P(('row', 'col'), 'feat')
- feature_grad: bfloat16 [65536, 256], P(('col', 'row'), 'feat')
- weight_grad: float32 [256, 256], P('feat')
Inputs may be any that keep to these rules, and one draw needn't show every extreme that they name: `tile_rows`: block rows of a cell, unevenly loaded. `tile_count`: some cell has all 256 slots live.
All inputs are finite; a program needn't handle non-finite values.
Results may differ from a plain program's by a relative error of at most 0.027.
Values may be sent and summed in bfloat16 or wider, within the bound.
A program may use at most 128 MiB of HBM per device.

v0:
```python
import jax
import jax.numpy as jnp
from jax import lax
from jax.sharding import PartitionSpec as P


def shards(features, tile_rows, tile_cols, tile_count, tile_values, weights, cotangent):
    width = tile_values.shape[-1]
    slots = tile_values.shape[2]
    local_tiles = tile_values[0, 0]
    block_rows = tile_rows[0, 0]
    block_cols = tile_cols[0, 0]
    live_mask = (jnp.arange(slots) < tile_count[0, 0]).astype(jnp.float32)
    n_rowdev = lax.axis_size("row")
    n_coldev = lax.axis_size("col")
    local_blocks = features.shape[0] // width
    feat_half = features.shape[1]
    feat_index = lax.axis_index("feat")
    row_blocks = local_blocks * n_coldev
    col_blocks = local_blocks * n_rowdev
    node_total = features.shape[0] * n_rowdev * n_coldev
    panel = lax.all_gather(features, "row", axis=0, tiled=True)
    gathered = panel.reshape(col_blocks, width, feat_half)[block_cols]
    products = jnp.einsum("tij,tjf->tif", local_tiles, gathered, preferred_element_type=jnp.float32)
    products = products * live_mask[:, None, None]
    partial_value = (
        jnp.zeros((row_blocks, width, feat_half), jnp.float32).at[block_rows].add(products)
    )
    summed = lax.psum_scatter(
        partial_value.reshape(row_blocks * width, feat_half).astype(jnp.bfloat16),
        "col",
        scatter_dimension=0,
        tiled=True,
    )
    weight_rows = lax.dynamic_slice_in_dim(weights, feat_index * feat_half, feat_half, 0)
    mix_term = jnp.dot(summed, weight_rows, preferred_element_type=jnp.float32)
    hidden = lax.psum_scatter(
        mix_term.astype(jnp.bfloat16), "feat", scatter_dimension=1, tiled=True
    ).astype(jnp.float32)
    negative = jnp.minimum(hidden, 0.0)
    activated = jnp.where(hidden > 0, hidden, jnp.expm1(negative)).astype(jnp.bfloat16)
    slope_factor = jnp.where(hidden > 0, 1.0, jnp.exp(negative))
    grad_out = (cotangent.astype(jnp.float32) * slope_factor).astype(jnp.bfloat16)
    grad_whole = lax.all_gather(grad_out, "feat", axis=1, tiled=True)
    weight_term = lax.dot_general(
        summed, grad_whole, (((0,), (0,)), ((), ())), preferred_element_type=jnp.float32
    )
    n_feat = lax.axis_size("feat")
    slots = jnp.zeros((n_feat,) + weight_term.shape, jnp.float32)
    slots = lax.dynamic_update_slice_in_dim(slots, weight_term[None], feat_index, 0)
    slots = lax.psum(slots, ("row", "col", "feat"))
    weight_grad = lax.dynamic_index_in_dim(slots, feat_index, 0, keepdims=False) * node_total ** (
        -0.5
    )
    spread = lax.dot_general(
        grad_whole, weight_rows, (((1,), (1,)), ((), ())), preferred_element_type=jnp.float32
    ).astype(jnp.bfloat16)
    spread_panel = lax.all_gather(spread, "col", axis=0, tiled=True)
    spread_blocks = spread_panel.reshape(row_blocks, width, feat_half)[block_rows]
    back_products = jnp.einsum(
        "tji,tjf->tif", local_tiles, spread_blocks, preferred_element_type=jnp.float32
    )
    back_products = back_products * live_mask[:, None, None]
    back_partial = (
        jnp.zeros((col_blocks, width, feat_half), jnp.float32).at[block_cols].add(back_products)
    )
    back_summed = lax.psum_scatter(
        back_partial.reshape(col_blocks * width, feat_half).astype(jnp.bfloat16),
        "row",
        scatter_dimension=0,
        tiled=True,
    )
    return (activated, back_summed, weight_grad)


def solution(mesh):
    return jax.shard_map(
        shards,
        mesh=mesh,
        in_specs=(
            P(("col", "row"), "feat"),
            P("row", "col", None),
            P("row", "col", None),
            P("row", "col"),
            P("row", "col", None, None, None),
            P(),
            P(("row", "col"), "feat"),
        ),
        out_specs=(P(("row", "col"), "feat"), P(("col", "row"), "feat"), P("feat", None)),
        check_vma=False,
    )
```

profile of v0, /device:TPU:2, one launch (start us, length us, event | category | flops | bytes accessed | tf_op | source)
XLA Modules:
  0.0 605.1 jit_solution(15216501221385841070)
XLA Ops:
  9.3 43.2 %all-gather.3.cloned.1.call-done = bf16[8192,128]{1,0:T(8,128)(2,1)} async-done(((bf16[512,128]{1,0:T(8,128)(2,1)}), bf16[8192,128]{1,0:T(8,128)(2,1)}) %all-gather.3.cloned.1.call-update) | async-done | bytes 2097168 | tf_op jit(solution)/shard_map/all_gather | solution.py:22
  52.6 10.2 %gather_fusion = bf16[256,128,128]{2,1,0:T(8,128)(2,1)} fusion(bf16[64,128,128]{2,1,0:T(8,128)(2,1)} %bitcast.36, s32[1024]{0:T(1024)S(1)} %pad_clamp_fusion.1), kind=kCustom, calls=%fused_computation | custom fusion | bytes 16778240 | tf_op jit(solution)/shard_map/gather | solution.py:23
  62.8 13.0 %multiply_bitcast_fusion.1 = f32[256,128,128]{1,2,0:T(8,128)} fusion(bf16[256,128,128]{2,1,0:T(8,128)(2,1)} %gather_fusion, bf16[1,1,256,128,128]{4,3,2,1,0:T(8,128)(2,1)} %param.11, f32[256]{0:T(256)S(1)} %compare_convert_fusion), kind=kOutput, calls=%fused_computation.5 | convolution fusion | flops 1077936128 | bytes 33555456 | tf_op jit(solution)/shard_map/tij,tjf->tif/dot_general | solution.py:24
  75.8 17.4 %copy.17 = f32[256,128,128]{2,1,0:T(8,128)} copy(f32[256,128,128]{1,2,0:T(8,128)} %multiply_bitcast_fusion.1) | data formatting | bytes 33554432 | tf_op jit(solution)/shard_map/mul | solution.py:25
  93.5 33.2 %scatter_fusion = f32[32,128,128]{2,1,0:T(8,128)S(1)} fusion(f32[32,128,128]{2,1,0:T(8,128)S(1)} %broadcast_in_dim.22, s32[256]{0:T(256)S(1)} %bitcast.43, f32[256,128,128]{2,1,0:T(8,128)} %copy.17), kind=kCustom, calls=%fused_computation.2 | custom fusion | flops 4194304 | bytes 50332672 | tf_op jit(solution)/shard_map/scatter-add | solution.py:27
  126.7 1.1 convert_element_type.38
  127.9 74.5 %reduce-scatter.6.cloned.1.call-done = bf16[512,128]{1,0:T(8,128)(2,1)} async-done(((bf16[4096,128]{1,0:T(8,128)(2,1)}), bf16[512,128]{1,0:T(8,128)(2,1)}) %reduce-scatter.6.cloned.1.call-update) | async-done | bytes 131088 | tf_op jit(solution)/shard_map/reduce_scatter | solution.py:29
  202.4 1.1 convolution_convert_fusion
  203.5 0.8 copy.22
  204.4 16.0 %reduce-scatter.10.cloned.1.call-done = bf16[128,512]{1,0:T(8,128)(2,1)} async-done(((bf16[256,512]{1,0:T(8,128)(2,1)}), bf16[128,512]{1,0:T(8,128)(2,1)}) %reduce-scatter.10.cloned.1.call-update) | async-done | bytes 131088
  220.4 1.0 copy.23
  222.3 5.9 all_gather.10
  228.2 0.9 convolution_convert_fusion.1
  229.2 1.1 fusion.2
  231.3 50.6 %all-gather.5.cloned.1.call-done = bf16[4096,128]{1,0:T(8,128)(2,1)} async-done(((bf16[512,128]{1,0:T(8,128)(2,1)}), bf16[4096,128]{1,0:T(8,128)(2,1)}) %all-gather.5.cloned.1.call-update) | async-done | bytes 1048592 | tf_op jit(solution)/shard_map/all_gather | solution.py:58
  281.9 9.8 %gather_fusion.1 = bf16[256,128,128]{2,1,0:T(8,128)(2,1)} fusion(bf16[32,128,128]{2,1,0:T(8,128)(2,1)} %bitcast.35, s32[1024]{0:T(1024)S(1)} %pad_clamp_fusion), kind=kCustom, calls=%fused_computation.1 | custom fusion | bytes 16778240 | tf_op jit(solution)/shard_map/gather | solution.py:59
  291.7 15.4 %multiply_bitcast_fusion = f32[256,128,128]{1,2,0:T(8,128)} fusion(bf16[256,128,128]{2,1,0:T(8,128)(2,1)} %gather_fusion.1, bf16[1,1,256,128,128]{4,3,2,1,0:T(8,128)(2,1)} %param.11, f32[256]{0:T(256)S(1)} %compare_convert_fusion), kind=kOutput, calls=%fused_computation.4 | convolution fusion | flops 1077936128 | bytes 33555456 | tf_op jit(solution)/shard_map/tji,tjf->tif/dot_general | solution.py:60
  307.1 17.5 %copy.19 = f32[256,128,128]{2,1,0:T(8,128)} copy(f32[256,128,128]{1,2,0:T(8,128)} %multiply_bitcast_fusion) | data formatting | bytes 33554432 | tf_op jit(solution)/shard_map/mul | solution.py:63
  324.6 2.5 broadcast_in_dim.23
  327.0 52.1 %scatter_fusion.1 = f32[64,128,128]{2,1,0:T(8,128)} fusion(f32[64,128,128]{2,1,0:T(8,128)} %broadcast_in_dim.23, s32[256]{0:T(256)S(1)} %bitcast.42, f32[256,128,128]{2,1,0:T(8,128)} %copy.19), kind=kCustom, calls=%fused_computation.3 | custom fusion | flops 4194304 | bytes 50332672 | tf_op jit(solution)/shard_map/scatter-add | solution.py:65
  379.1 3.9 convert_element_type.46
  383.1 154.2 %all-reduce.2.cloned.1.call-done = f32[2,128,256]{2,1,0:T(8,128)} async-done(((f32[2,128,256]{2,1,0:T(8,128)}), f32[2,128,256]{2,1,0:T(8,128)}) %all-reduce.2.cloned.1.call-update) | async-done | bytes 262160 | tf_op jit(solution)/shard_map/psum | solution.py:51
  537.3 1.6 multiply_bitcast_fusion.2
  538.8 59.4 %reduce-scatter.8.cloned.1.call-done = bf16[512,128]{1,0:T(8,128)(2,1)} async-done(((bf16[8192,128]{1,0:T(8,128)(2,1)}), bf16[512,128]{1,0:T(8,128)(2,1)}) %reduce-scatter.8.cloned.1.call-update) | async-done | bytes 131088 | tf_op jit(solution)/shard_map/reduce_scatter | solution.py:67
  (27 shorter events, 3.7 us)
Async XLA Ops:
  7.2 195.2 %copy-start = (bf16[256,256]{1,0:T(8,128)(2,1)S(1)}, bf16[256,256]{1,0:T(8,128)(2,1)}, u32[]{:S(2)}) copy-start(bf16[256,256]{1,0:T(8,128)(2,1)} %param.12) | copy-start | bytes 393220
  7.2 45.4 %all-gather.3.cloned.1.call-start = ((), (), s32[]{:S(2)}) async-start(), calls=%async_computation.3 | async-start | bytes 2228224 | tf_op jit(solution)/shard_map/all_gather | solution.py:22
  7.9 194.4 %reduce-scatter.6.cloned.1.call-start = ((), (), s32[]{:S(2)}) async-start(), calls=%async_computation.4 | async-start | bytes 1179648 | tf_op jit(solution)/shard_map/reduce_scatter | solution.py:29
  93.5 128.0 %copy-start.3 = (bf16[512,128]{1,0:T(8,128)(2,1)S(1)}, bf16[512,128]{1,0:T(8,128)(2,1)}, u32[]{:S(2)}) copy-start(bf16[512,128]{1,0:T(8,128)(2,1)} %param.13) | copy-start | bytes 393220
  127.8 92.6 %reduce-scatter.10.cloned.1.call-start = ((), (), s32[]{:S(2)}) async-start(), calls=%async_computation.8 | async-start | bytes 393216
  204.3 77.5 %all-gather.5.cloned.1.call-start = ((), (), s32[]{:S(2)}) async-start(), calls=%async_computation.5 | async-start | bytes 1179648 | tf_op jit(solution)/shard_map/all_gather | solution.py:58
  229.1 308.2 %all-reduce.2.cloned.1.call-start = ((), (), s32[]{:S(2)}) async-start(), calls=%async_computation.7 | async-start | bytes 524288 | tf_op jit(solution)/shard_map/psum | solution.py:51
  230.3 0.7 copy-start.2
  231.0 367.2 %reduce-scatter.8.cloned.1.call-start = ((), (), s32[]{:S(2)}) async-start(), calls=%async_computation.6 | async-start | bytes 2228224 | tf_op jit(solution)/shard_map/reduce_scatter | solution.py:67
  327.0 271.2 %copy-start.1 = (bf16[256,256]{1,0:T(8,128)(2,1)S(1)}, bf16[256,256]{1,0:T(8,128)(2,1)}, u32[]{:S(2)}) copy-start(bf16[256,256]{1,0:T(8,128)(2,1)} %param.12) | copy-start | bytes 393220
Sparse Core Ops, SparseCore 0:
  9.8 42.6 all-gather.2
  127.9 74.3 reduce-scatter.5
  205.0 15.3 reduce-scatter.9
  229.2 52.6 all-gather.4
  287.2 250.0 all-reduce.1
  540.2 57.9 reduce-scatter.7
where the time goes:
time: 607 us; the launch traced here: 605 us
  waiting for transfers between devices  399 us (66%)
  other arithmetic  93.4 us (15%)
  local copies, waits for them, and re-layouts  60.2 us (10%)
  matrix products  31.5 us (5%)
  between operations  14.9 us (2%)
    psum x1, waiting for transfers between devices, shards(): slots = lax.psum(slots, ('row', 'col', 'feat'))  154 us
    reduce_scatter x1, waiting for transfers between devices, shards(): lax.psum_scatter(partial_value.reshape(row_blocks * width, feat_half).ast...  74.5 us
    reduce_scatter x1, waiting for transfers between devices, shards(): lax.psum_scatter(back_partial.reshape(col_blocks * width, feat_half).asty...  59.4 us
    scatter-add x1, other arithmetic, shards(): jnp.zeros((col_blocks, width, feat_half), jnp.float32).at[block_cols]  52.1 us
    all_gather x1, waiting for transfers between devices, shards(): spread_panel = lax.all_gather(spread, 'col', axis=0, tiled=True)  50.6 us
    all_gather x1, waiting for transfers between devices, shards(): panel = lax.all_gather(features, 'row', axis=0, tiled=True)  43.2 us
    scatter-add x1, other arithmetic, shards(): jnp.zeros((row_blocks, width, feat_half), jnp.float32).at[block_rows]  33.2 us
    mul x1, local copies, waits for them, and re-layouts, shards(): back_products = back_products * live_mask[:, None, None]  17.5 us
  transfers between devices with their start and end apart: 6, of which 6 were waited for; matrix products, arithmetic and copies ran while one was open for 17% of the time, Pallas kernels for 0%

commit v1 on v0

--- a/solution.py
+++ b/solution.py
@@ -2,6 +2,11 @@
 import jax.numpy as jnp
 from jax import lax
 from jax.sharding import PartitionSpec as P
+
+
+def by_each_axis(value, first, second):
+    half = lax.psum(value, first)
+    return lax.psum(half, second)
 
 
 def shards(features, tile_rows, tile_cols, tile_count, tile_values, weights, cotangent):
@@ -48,7 +53,7 @@
     n_feat = lax.axis_size("feat")
     slots = jnp.zeros((n_feat,) + weight_term.shape, jnp.float32)
     slots = lax.dynamic_update_slice_in_dim(slots, weight_term[None], feat_index, 0)
-    slots = lax.psum(slots, ("row", "col", "feat"))
+    slots = by_each_axis(slots, "row", ("col", "feat"))
     weight_grad = lax.dynamic_index_in_dim(slots, feat_index, 0, keepdims=False) * node_total ** (
         -0.5
     )

time: 607 us -> 564 us (0.929)
  waiting for transfers between devices: 399 us -> 356 us
    psum x1 -> x2, waiting for transfers between devices: 154 us -> 110 us  [the longest x1 110 us: by_each_axis(): half = lax.psum(value, first)]
    unnamed x7 -> x8, waiting for transfers between devices: 16.8 us -> 16.8 us
  transfers between devices with their start and end apart: 6 -> 7, of which waited for: 6 -> 6; matrix products, arithmetic and copies ran while one was open for 17% -> 19% of each run, Pallas kernels for 0% -> 0%
where the time goes in v1:
time: 564 us; the launch traced here: 562 us
  waiting for transfers between devices  356 us (63%)
  other arithmetic  93.4 us (17%)
  local copies, waits for them, and re-layouts  60.2 us (11%)
  matrix products  31.6 us (6%)
  between operations  14.9 us (3%)
  blocking collectives  5.89 us (1%)
    psum x1, waiting for transfers between devices, by_each_axis(): half = lax.psum(value, first)  110 us
    reduce_scatter x1, waiting for transfers between devices, shards(): lax.psum_scatter(partial_value.reshape(row_blocks * width, feat_half).ast...  74.5 us
    reduce_scatter x1, waiting for transfers between devices, shards(): lax.psum_scatter(back_partial.reshape(col_blocks * width, feat_half).asty...  57.5 us
    all_gather x1, waiting for transfers between devices, shards(): spread_panel = lax.all_gather(spread, 'col', axis=0, tiled=True)  54.1 us
    scatter-add x1, other arithmetic, shards(): jnp.zeros((col_blocks, width, feat_half), jnp.float32).at[block_cols]  52 us
    all_gather x1, waiting for transfers between devices, shards(): panel = lax.all_gather(features, 'row', axis=0, tiled=True)  43.2 us
    scatter-add x1, other arithmetic, shards(): jnp.zeros((row_blocks, width, feat_half), jnp.float32).at[block_rows]  33.2 us
    mul x1, local copies, waits for them, and re-layouts, shards(): back_products = back_products * live_mask[:, None, None]  17.5 us
  transfers between devices with their start and end apart: 7, of which 6 were waited for; matrix products, arithmetic and copies ran while one was open for 19% of the time, Pallas kernels for 0%

profile of v1, /device:TPU:2, one launch (start us, length us, event | category | flops | bytes accessed | tf_op | source)
XLA Modules:
  0.0 562.3 jit_solution(4279256555704040123)
XLA Ops:
  9.3 43.2 %all-gather.3.cloned.1.call-done = bf16[8192,128]{1,0:T(8,128)(2,1)} async-done(((bf16[512,128]{1,0:T(8,128)(2,1)}), bf16[8192,128]{1,0:T(8,128)(2,1)}) %all-gather.3.cloned.1.call-update) | async-done | bytes 2097168 | tf_op jit(solution)/shard_map/all_gather | solution.py:27
  52.6 10.2 %gather_fusion = bf16[256,128,128]{2,1,0:T(8,128)(2,1)} fusion(bf16[64,128,128]{2,1,0:T(8,128)(2,1)} %bitcast.36, s32[1024]{0:T(1024)S(1)} %pad_clamp_fusion.1), kind=kCustom, calls=%fused_computation | custom fusion | bytes 16778240 | tf_op jit(solution)/shard_map/gather | solution.py:28
  62.8 13.0 %multiply_bitcast_fusion.1 = f32[256,128,128]{1,2,0:T(8,128)} fusion(bf16[256,128,128]{2,1,0:T(8,128)(2,1)} %gather_fusion, bf16[1,1,256,128,128]{4,3,2,1,0:T(8,128)(2,1)} %param.11, f32[256]{0:T(256)S(1)} %compare_convert_fusion), kind=kOutput, calls=%fused_computation.5 | convolution fusion | flops 1077936128 | bytes 33555456 | tf_op jit(solution)/shard_map/tij,tjf->tif/dot_general | solution.py:29
  75.8 17.4 %copy.17 = f32[256,128,128]{2,1,0:T(8,128)} copy(f32[256,128,128]{1,2,0:T(8,128)} %multiply_bitcast_fusion.1) | data formatting | bytes 33554432 | tf_op jit(solution)/shard_map/mul | solution.py:30
  93.5 33.2 %scatter_fusion = f32[32,128,128]{2,1,0:T(8,128)S(1)} fusion(f32[32,128,128]{2,1,0:T(8,128)S(1)} %broadcast_in_dim.22, s32[256]{0:T(256)S(1)} %bitcast.43, f32[256,128,128]{2,1,0:T(8,128)} %copy.17), kind=kCustom, calls=%fused_computation.2 | custom fusion | flops 4194304 | bytes 50332672 | tf_op jit(solution)/shard_map/scatter-add | solution.py:32
  126.7 1.1 convert_element_type.38
  127.9 74.5 %reduce-scatter.6.cloned.1.call-done = bf16[512,128]{1,0:T(8,128)(2,1)} async-done(((bf16[4096,128]{1,0:T(8,128)(2,1)}), bf16[512,128]{1,0:T(8,128)(2,1)}) %reduce-scatter.6.cloned.1.call-update) | async-done | bytes 131088 | tf_op jit(solution)/shard_map/reduce_scatter | solution.py:34
  202.4 1.1 convolution_convert_fusion
  203.5 0.8 copy.22
  204.4 16.0 %reduce-scatter.10.cloned.1.call-done = bf16[128,512]{1,0:T(8,128)(2,1)} async-done(((bf16[256,512]{1,0:T(8,128)(2,1)}), bf16[128,512]{1,0:T(8,128)(2,1)}) %reduce-scatter.10.cloned.1.call-update) | async-done | bytes 131088
  220.4 1.0 copy.23
  222.3 5.9 %all_gather.10 = bf16[512,256]{1,0:T(8,128)(2,1)S(1)} all-gather(bf16[512,128]{1,0:T(8,128)(2,1)S(1)} %get-tuple-element.3), channel_id=1, replica_groups=mesh['row'=16,'col'=8,'feat'=2] {'feat'}, dimensions={1}, use_global_device_ids=true | all-gather | bytes 393216 | tf_op jit(solution)/shard_map/all_gather | solution.py:49
  228.2 1.1 fusion.2
  230.1 0.9 convolution_convert_fusion.1
  231.1 109.8 %all-reduce.3.cloned.1.call-done = f32[2,128,256]{2,1,0:T(8,128)} async-done(((f32[2,128,256]{2,1,0:T(8,128)}), f32[2,128,256]{2,1,0:T(8,128)}) %all-reduce.3.cloned.1.call-update) | async-done | bytes 262160 | tf_op jit(solution)/shard_map/psum | solution.py:8
  341.1 54.1 %all-gather.5.cloned.1.call-done = bf16[4096,128]{1,0:T(8,128)(2,1)} async-done(((bf16[512,128]{1,0:T(8,128)(2,1)}), bf16[4096,128]{1,0:T(8,128)(2,1)}) %all-gather.5.cloned.1.call-update) | async-done | bytes 1048592 | tf_op jit(solution)/shard_map/all_gather | solution.py:63
  395.2 9.8 %gather_fusion.1 = bf16[256,128,128]{2,1,0:T(8,128)(2,1)} fusion(bf16[32,128,128]{2,1,0:T(8,128)(2,1)} %bitcast.35, s32[1024]{0:T(1024)S(1)} %pad_clamp_fusion), kind=kCustom, calls=%fused_computation.1 | custom fusion | bytes 16778240 | tf_op jit(solution)/shard_map/gather | solution.py:64
  405.0 15.5 %multiply_bitcast_fusion = f32[256,128,128]{1,2,0:T(8,128)} fusion(bf16[256,128,128]{2,1,0:T(8,128)(2,1)} %gather_fusion.1, bf16[1,1,256,128,128]{4,3,2,1,0:T(8,128)(2,1)} %param.11, f32[256]{0:T(256)S(1)} %compare_convert_fusion), kind=kOutput, calls=%fused_computation.4 | convolution fusion | flops 1077936128 | bytes 33555456 | tf_op jit(solution)/shard_map/tji,tjf->tif/dot_general | solution.py:65
  420.5 17.5 %copy.19 = f32[256,128,128]{2,1,0:T(8,128)} copy(f32[256,128,128]{1,2,0:T(8,128)} %multiply_bitcast_fusion) | data formatting | bytes 33554432 | tf_op jit(solution)/shard_map/mul | solution.py:68
  437.9 2.5 broadcast_in_dim.23
  440.4 52.0 %scatter_fusion.1 = f32[64,128,128]{2,1,0:T(8,128)} fusion(f32[64,128,128]{2,1,0:T(8,128)} %broadcast_in_dim.23, s32[256]{0:T(256)S(1)} %bitcast.42, f32[256,128,128]{2,1,0:T(8,128)} %copy.19), kind=kCustom, calls=%fused_computation.3 | custom fusion | flops 4194304 | bytes 50332672 | tf_op jit(solution)/shard_map/scatter-add | solution.py:70
  492.4 3.9 convert_element_type.46
  496.4 1.6 multiply_bitcast_fusion.2
  498.0 57.5 %reduce-scatter.8.cloned.1.call-done = bf16[512,128]{1,0:T(8,128)(2,1)} async-done(((bf16[8192,128]{1,0:T(8,128)(2,1)}), bf16[512,128]{1,0:T(8,128)(2,1)}) %reduce-scatter.8.cloned.1.call-update) | async-done | bytes 131088 | tf_op jit(solution)/shard_map/reduce_scatter | solution.py:72
  (30 shorter events, 3.7 us)
Async XLA Ops:
  7.2 195.2 %copy-start = (bf16[256,256]{1,0:T(8,128)(2,1)S(1)}, bf16[256,256]{1,0:T(8,128)(2,1)}, u32[]{:S(2)}) copy-start(bf16[256,256]{1,0:T(8,128)(2,1)} %param.12) | copy-start | bytes 393220
  7.2 45.4 %all-gather.3.cloned.1.call-start = ((), (), s32[]{:S(2)}) async-start(), calls=%async_computation.3 | async-start | bytes 2228224 | tf_op jit(solution)/shard_map/all_gather | solution.py:27
  7.9 194.4 %reduce-scatter.6.cloned.1.call-start = ((), (), s32[]{:S(2)}) async-start(), calls=%async_computation.4 | async-start | bytes 1179648 | tf_op jit(solution)/shard_map/reduce_scatter | solution.py:34
  93.5 128.0 %copy-start.3 = (bf16[512,128]{1,0:T(8,128)(2,1)S(1)}, bf16[512,128]{1,0:T(8,128)(2,1)}, u32[]{:S(2)}) copy-start(bf16[512,128]{1,0:T(8,128)(2,1)} %param.13) | copy-start | bytes 393220
  127.8 92.6 %reduce-scatter.10.cloned.1.call-start = ((), (), s32[]{:S(2)}) async-start(), calls=%async_computation.9 | async-start | bytes 393216
  204.3 136.5 %all-reduce.3.cloned.1.call-start = ((), (), s32[]{:S(2)}) async-start(), calls=%async_computation.7 | async-start | bytes 524288 | tf_op jit(solution)/shard_map/psum | solution.py:8
  229.3 0.7 copy-start.2
  230.0 165.2 %all-gather.5.cloned.1.call-start = ((), (), s32[]{:S(2)}) async-start(), calls=%async_computation.5 | async-start | bytes 1179648 | tf_op jit(solution)/shard_map/all_gather | solution.py:63
  231.0 265.4 %all-reduce.5.cloned.1.call-start = ((), (), s32[]{:S(2)}) async-start(), calls=%async_computation.8 | async-start | bytes 524288 | tf_op jit(solution)/shard_map/psum | solution.py:9
  340.9 214.5 %reduce-scatter.8.cloned.1.call-start = ((), (), s32[]{:S(2)}) async-start(), calls=%async_computation.6 | async-start | bytes 2228224 | tf_op jit(solution)/shard_map/reduce_scatter | solution.py:72
  440.4 115.0 %copy-start.1 = (bf16[256,256]{1,0:T(8,128)(2,1)S(1)}, bf16[256,256]{1,0:T(8,128)(2,1)}, u32[]{:S(2)}) copy-start(bf16[256,256]{1,0:T(8,128)(2,1)} %param.12) | copy-start | bytes 393220
Sparse Core Ops, SparseCore 0:
  9.8 42.6 all-gather.2
  127.9 74.3 reduce-scatter.5
  205.0 15.3 reduce-scatter.9
  230.2 110.6 all-reduce.2
  344.3 50.8 all-gather.4
  398.5 93.7 all-reduce.4
  496.5 58.8 reduce-scatter.7
